TPU v7x, 128 devices: a whole 4x4x4 slice. The times are simulated.
128 devices in a mesh: section: 8 (over x, core), seq: 16 (over z, y).
Axes of the slice: x: 4, y: 4, z: 4, core: 2. Of those that a mesh axis runs over, the one named last changes fastest.
Arguments:
- residual: bfloat16 [8, 4096, 2048], P('section', 'seq'), may hold values from -6 to 6
- w_qkv: bfloat16 [8, 2048, 6144], P('section', 'seq'), may hold values from -0.125 to 0.125
- w_beta: bfloat16 [8, 2048, 16], P('section', 'seq'), may hold values from -0.125 to 0.125
- beta_bias: float32 [8, 16], P('section'), may hold values from -8 to 2
- norm_gain: float32 [8, 2048], P('section'), may hold values from 0.1 to 1.9
- out_gain: float32 [8, 128], P('section'), may hold values from 0.1 to 1.9
- state_in: float32 [8, 16, 128, 128], P('section'), may hold values from -6 to 6
- doc_start: int32 [2, 8], P(None, 'section'), may hold values from 0 to 64, as said below
Outputs:
- stream_out: bfloat16 [8, 4096, 2048], P('section', 'seq')
Inputs may be any that keep to these rules, and one draw needn't show every extreme that they name: `doc_start`: 64 means no new document in that micro-batch.
All inputs are finite; a program needn't handle non-finite values.
Results may differ from a plain program's by a relative error of at most 0.03.
Values may be sent and summed in bfloat16 or wider, within the bound.
No kernel may reach another device: no remote copies, remote signals or barrier semaphores. Data moves between devices by JAX's collectives and lax.ppermute only.
A program may use at most 192 MiB of HBM per device.

v0:
```python
import jax
import jax.numpy as jnp
from jax import lax
from jax.sharding import PartitionSpec as P

HEADS = 16
HD = 128
GROUP = 64
TICKS = 2
FULL_PRECISION = lax.Precision.HIGHEST


def from_behind(value, axis, by):
    count = lax.axis_size(axis)
    pairs = [(i, i + by) for i in range(count) if 0 <= i + by < count]
    return lax.ppermute(value, axis, pairs)


def from_root(value, axis, source):
    kept = jnp.where(lax.axis_index(axis) == source, value, 0).astype(value.dtype)
    return lax.psum(kept, axis)


def passed_along(value, axis, by):
    count = lax.axis_size(axis)
    return lax.ppermute(value, axis, [(i, (i + by) % count) for i in range(count)])


def unit_norm(projected):
    return projected * lax.rsqrt(jnp.sum(projected * projected, axis=-1, keepdims=True) + 1e-06)


def block_solve(key_rows, values, beta_rows):
    block_len = key_rows.shape[-2]
    intersections = jnp.einsum("ghik,ghjk->ghij", key_rows, key_rows, precision=FULL_PRECISION)
    system = jnp.tril(intersections * beta_rows[..., :, None], -1) + jnp.eye(
        block_len, dtype=jnp.float32
    )
    right_side = jnp.concatenate(
        [values * beta_rows[..., None], key_rows * beta_rows[..., None]], axis=-1
    )
    solved = lax.linalg.triangular_solve(
        system, right_side, left_side=True, lower=True, unit_diagonal=True
    )
    head_width = values.shape[-1]
    return (solved[..., :head_width], solved[..., head_width:])


def prepare(stream, weight_qkv, weight_beta, head_bias, in_gain):
    row_count = stream.shape[0]
    widened = stream.astype(jnp.float32)
    normed = (
        widened * lax.rsqrt(jnp.mean(widened * widened, axis=-1, keepdims=True) + 1e-05) * in_gain
    ).astype(jnp.bfloat16)
    projected = jnp.dot(normed, weight_qkv, preferred_element_type=jnp.float32).reshape(
        row_count, 3, HEADS, HD
    )
    queries = unit_norm(projected[:, 0]).astype(jnp.bfloat16)
    key_rows = unit_norm(projected[:, 1]).astype(jnp.bfloat16)
    values = projected[:, 2].astype(jnp.bfloat16)
    beta_rows = jax.nn.sigmoid(
        jnp.dot(normed, weight_beta, preferred_element_type=jnp.float32) + head_bias
    )
    blocks = row_count // GROUP

    def to_blocks(tensor):
        return tensor.astype(jnp.float32).reshape(blocks, GROUP, HEADS, HD).transpose(0, 2, 1, 3)

    beta_blk = beta_rows.reshape(blocks, GROUP, HEADS).transpose(0, 2, 1)
    key_block = to_blocks(key_rows)
    inject, weights = block_solve(key_block, to_blocks(values), beta_blk)
    return (to_blocks(queries), key_block, inject, weights, widened)


def run_blocks(queries, key_rows, inject, weights, current_state, doc_block, first_block):
    block_count = queries.shape[0]
    block_len = queries.shape[2]
    causal = jnp.tril(jnp.ones((block_len, block_len), jnp.float32))

    def run_advance(current_state, pieces):
        query_block, key_block, inject_block, weight_block, block_index = pieces
        current_state = jnp.where(
            block_index == doc_block, jnp.zeros_like(current_state), current_state
        )
        delta_values = inject_block - jnp.einsum(
            "jxy,jyu->jxu", weight_block, current_state, precision=FULL_PRECISION
        )
        attention_scores = (
            jnp.einsum("hik,hjk->hij", query_block, key_block, precision=FULL_PRECISION) * causal
        )
        block_result = jnp.einsum(
            "jxy,jyu->jxu", query_block, current_state, precision=FULL_PRECISION
        ) + jnp.einsum("ucd,udo->uco", attention_scores, delta_values, precision=FULL_PRECISION)
        current_state = current_state + jnp.einsum(
            "plq,plw->pqw", key_block, delta_values, precision=FULL_PRECISION
        )
        return (current_state, block_result)

    block_ids = first_block + jnp.arange(block_count, dtype=jnp.int32)
    return lax.scan(run_advance, current_state, (queries, key_rows, inject, weights, block_ids))


def transitions(key_rows, inject, weights, doc_block, first_block):
    head_count = key_rows.shape[1]
    head_width = key_rows.shape[3]
    block_count = key_rows.shape[0]
    identity = jnp.broadcast_to(
        jnp.eye(head_width, dtype=jnp.float32), (head_count, head_width, head_width)
    )

    def transitions_advance(maps, pieces):
        decay_matrix, start_offset = maps
        key_block, inject_block, weight_block, block_index = pieces
        keep_flag = block_index != doc_block
        decay_matrix = jnp.where(keep_flag, decay_matrix, jnp.zeros_like(decay_matrix))
        start_offset = jnp.where(keep_flag, start_offset, jnp.zeros_like(start_offset))
        decay_matrix = decay_matrix - jnp.einsum(
            "plq,plw->pqw",
            key_block,
            jnp.einsum("jxy,jyu->jxu", weight_block, decay_matrix, precision=FULL_PRECISION),
            precision=FULL_PRECISION,
        )
        start_offset = start_offset + jnp.einsum(
            "plq,plw->pqw",
            key_block,
            inject_block
            - jnp.einsum("jxy,jyu->jxu", weight_block, start_offset, precision=FULL_PRECISION),
            precision=FULL_PRECISION,
        )
        return ((decay_matrix, start_offset), None)

    block_ids = first_block + jnp.arange(block_count, dtype=jnp.int32)
    maps, unused = lax.scan(
        transitions_advance,
        (identity, jnp.zeros_like(identity)),
        (key_rows, inject, weights, block_ids),
    )
    return maps


def apply_map(maps, given_state):
    return jnp.einsum("hij,hjk->hik", maps[0], given_state, precision=FULL_PRECISION) + maps[1]


def compose(earlier, latter):
    return (
        jnp.einsum("hij,hjk->hik", latter[0], earlier[0], precision=FULL_PRECISION),
        jnp.einsum("hij,hjk->hik", latter[0], earlier[1], precision=FULL_PRECISION) + latter[1],
    )


def finish(widened, block_result, head_gain):
    blocks = block_result.shape[0]
    mixed = block_result.transpose(0, 2, 1, 3).reshape(blocks * GROUP, HEADS, HD)
    mixed = mixed * lax.rsqrt(jnp.mean(mixed * mixed, axis=-1, keepdims=True) + 1e-05) * head_gain
    return (widened + mixed.reshape(blocks * GROUP, HEADS * HD)).astype(jnp.bfloat16)


def shards(residual, w_qkv, w_beta, beta_bias, norm_gain, out_gain, state_in, doc_start):
    weight_qkv, weight_beta = (
        lax.all_gather(w_qkv[0], "seq", axis=0, tiled=True),
        lax.all_gather(w_beta[0], "seq", axis=0, tiled=True),
    )
    seq_count = lax.axis_size("seq")
    position = lax.axis_index("seq")
    stream = residual[0]
    given_state = state_in[0]
    blocks = stream.shape[0] // GROUP
    first_block = position * blocks
    outputs = stream
    identity = jnp.broadcast_to(jnp.eye(HD, dtype=jnp.float32), (HEADS, HD, HD))
    empty_map = jnp.stack([identity, jnp.zeros_like(identity)])
    for tick_index in range(TICKS):
        doc_block = doc_start[tick_index, 0]
        queries, key_rows, inject, weights, widened = prepare(
            stream, weight_qkv, weight_beta, beta_bias[0], norm_gain[0]
        )
        maps = transitions(key_rows, inject, weights, doc_block, first_block)

        def hop_once(hop_index, carried_map):
            joined = compose((carried_map[0], carried_map[1]), maps)
            passed = from_behind(
                jnp.stack([joined[0], joined[1]]).astype(jnp.bfloat16), "seq", 1
            ).astype(jnp.float32)
            return jnp.where(position == 0, empty_map, passed)

        prefix_map = lax.fori_loop(0, seq_count - 1, hop_once, empty_map)
        prefix = (prefix_map[0], prefix_map[1])
        entry_state = apply_map(prefix, given_state)
        final_state, block_result = run_blocks(
            queries, key_rows, inject, weights, entry_state, doc_block, first_block
        )
        outputs = finish(widened, block_result, out_gain[0])
        if tick_index + 1 < TICKS:
            given_state = from_root(final_state.astype(jnp.bfloat16), "seq", seq_count - 1).astype(
                final_state.dtype
            )
            stream = passed_along(outputs, "section", 1)
    return outputs[None]


def solution(mesh):
    return jax.shard_map(
        shards,
        mesh=mesh,
        in_specs=(
            P("section", "seq", None),
            P("section", "seq", None),
            P("section", "seq", None),
            P("section", None),
            P("section", None),
            P("section", None),
            P("section", None, None, None),
            P(None, "section"),
        ),
        out_specs=P("section", "seq", None),
        check_vma=False,
    )
```

profile of v0, /device:TPU:34, one launch (start us, length us, event | category | flops | bytes accessed | tf_op | source)
XLA Modules:
  0.0 2081.2 jit_solution(3336317457587673220)
XLA Ops:
  7.3 24.4 %all-gather.1 = bf16[1,2048,16]{1,2,0:T(8,128)(2,1)S(1)} all-gather(bf16[1,128,16]{1,2,0:T(8,128)(2,1)} %param.24), channel_id=3, replica_groups=mesh['section'=8,'seq'=16] {'seq'}, dimensions={1}, use_global_device_ids=true | all-gather | bytes 69632 | tf_op jit(solution)/shard_map/all_gather | solution.py:162
  35.8 130.0 %all-gather.4.cloned.1.call-done = bf16[1,2048,6144]{2,1,0:T(8,128)(2,1)} async-done(((bf16[1,128,6144]{2,1,0:T(8,128)(2,1)}), bf16[1,2048,6144]{2,1,0:T(8,128)(2,1)}) %all-gather.4.cloned.1.call-update) | async-done | bytes 25165840 | tf_op jit(solution)/shard_map/all_gather | solution.py:161
  165.8 29.7 %copy.95 = bf16[6144,2048]{1,0:T(8,128)(2,1)} copy(bf16[6144,2048]{0,1:T(8,128)(2,1)} %bitcast.357) | data formatting | bytes 50331648 | tf_op jit(solution)/shard_map/dot_general | solution.py:55
  195.5 11.4 fusion.150
  209.8 4.0 broadcast_multiply_fusion.1
  217.8 316.0 %custom-call.6 = f32[4,16,1,64,64]{3,4,2,1,0:T(8,128)} custom-call(f32[4,16,1,64,64]{4,3,2,1,0:T(8,128)} %add_bitcast_fusion.1), custom_call_target="InvertDiagBlocksLowerTriangular" | custom-call | tf_op jit(solution)/shard_map/triangular_solve/custom-call.1 | solution.py:42
  533.8 6.6 fusion.107
  543.2 41.3 %while.80 = (s32[]{:T(128)}, f32[16,128,128]{2,1,0:T(8,128)S(1)}, f32[16,128,128]{2,1,0:T(8,128)S(1)}, s32[4]{0:T(128)S(1)}, s32[]{:T(128)}, /*index=5*/f32[4,16...) while((s32[]{:T(128)}, f32[16,128,128]{2,1,0:T(8,128)S(1)}, ...), condition=%wide.region_3.5_spmd.clone, body=%wide.region_2.4_spmd.clone.sunk | while | flops 807534592 | bytes 19400364 | solution.py:133
  584.6 464.3 %while.76 = (s32[]{:T(128)}, f32[2,16,128,128]{3,2,1,0:T(8,128)}, pred[]{:T(512)}, f32[16,128,128]{2,1,0:T(8,128)S(1)}, f32[16,128,128]{2,1,0:T(8,128)S(1)}, /*index=5*/f32[2,16,128,128]{3,2,1,0:T(8,128)}, s32[]{:T(128)}) while((s32[]{:T(128)}, f32[2,16,128,128]{3,2,1,0:T(8,128)}, pred[]{:T(512)}, f32[16,128,128]{2,1,0:T(8,128)S(1)}, ...), condition=%wide.region_5.7_spmd, body=%wide.region_4.6_spmd.sunk | while | flops 807665664 | bytes 26214544 | solution.py:187
  591.6 27.0 %collective-permute-done = bf16[2,16,128,128]{3,2,1,0:T(8,128)(2,1)} collective-permute-done((bf16[2,16,128,128]{3,2,1,0:T(8,128)(2,1)}, bf16[2,16,128,128]{3,2,1,0:T(8,128)(2,1)}, u32[]{:S(2)}, u32[]{:S(2)}) %collective-permute-start) | collective-permute-done | bytes 1048608 | tf_op jit(solution)/shard_map/while/body/eval_jaxpr/ppermute | solution.py:16
  628.4 26.4 %collective-permute-done = bf16[2,16,128,128]{3,2,1,0:T(8,128)(2,1)} collective-permute-done((bf16[2,16,128,128]{3,2,1,0:T(8,128)(2,1)}, bf16[2,16,128,128]{3,2,1,0:T(8,128)(2,1)}, u32[]{:S(2)}, u32[]{:S(2)}) %collective-permute-start) | collective-permute-done | bytes 1048608 | tf_op jit(solution)/shard_map/while/body/eval_jaxpr/ppermute | solution.py:16
  654.8 3.0 convert_select_fusion.5
  664.5 25.5 %collective-permute-done = bf16[2,16,128,128]{3,2,1,0:T(8,128)(2,1)} collective-permute-done((bf16[2,16,128,128]{3,2,1,0:T(8,128)(2,1)}, bf16[2,16,128,128]{3,2,1,0:T(8,128)(2,1)}, u32[]{:S(2)}, u32[]{:S(2)}) %collective-permute-start) | collective-permute-done | bytes 1048608 | tf_op jit(solution)/shard_map/while/body/eval_jaxpr/ppermute | solution.py:16
  690.0 3.0 convert_select_fusion.5
  699.7 24.6 %collective-permute-done = bf16[2,16,128,128]{3,2,1,0:T(8,128)(2,1)} collective-permute-done((bf16[2,16,128,128]{3,2,1,0:T(8,128)(2,1)}, bf16[2,16,128,128]{3,2,1,0:T(8,128)(2,1)}, u32[]{:S(2)}, u32[]{:S(2)}) %collective-permute-start) | collective-permute-done | bytes 1048608 | tf_op jit(solution)/shard_map/while/body/eval_jaxpr/ppermute | solution.py:16
  724.3 3.0 convert_select_fusion.5
  734.0 23.6 %collective-permute-done = bf16[2,16,128,128]{3,2,1,0:T(8,128)(2,1)} collective-permute-done((bf16[2,16,128,128]{3,2,1,0:T(8,128)(2,1)}, bf16[2,16,128,128]{3,2,1,0:T(8,128)(2,1)}, u32[]{:S(2)}, u32[]{:S(2)}) %collective-permute-start) | collective-permute-done | bytes 1048608 | tf_op jit(solution)/shard_map/while/body/eval_jaxpr/ppermute | solution.py:16
  757.6 3.0 convert_select_fusion.5
  767.3 22.7 %collective-permute-done = bf16[2,16,128,128]{3,2,1,0:T(8,128)(2,1)} collective-permute-done((bf16[2,16,128,128]{3,2,1,0:T(8,128)(2,1)}, bf16[2,16,128,128]{3,2,1,0:T(8,128)(2,1)}, u32[]{:S(2)}, u32[]{:S(2)}) %collective-permute-start) | collective-permute-done | bytes 1048608 | tf_op jit(solution)/shard_map/while/body/eval_jaxpr/ppermute | solution.py:16
  790.0 3.0 convert_select_fusion.5
  799.8 21.8 %collective-permute-done = bf16[2,16,128,128]{3,2,1,0:T(8,128)(2,1)} collective-permute-done((bf16[2,16,128,128]{3,2,1,0:T(8,128)(2,1)}, bf16[2,16,128,128]{3,2,1,0:T(8,128)(2,1)}, u32[]{:S(2)}, u32[]{:S(2)}) %collective-permute-start) | collective-permute-done | bytes 1048608 | tf_op jit(solution)/shard_map/while/body/eval_jaxpr/ppermute | solution.py:16
  821.6 3.0 convert_select_fusion.5
  831.3 20.9 %collective-permute-done = bf16[2,16,128,128]{3,2,1,0:T(8,128)(2,1)} collective-permute-done((bf16[2,16,128,128]{3,2,1,0:T(8,128)(2,1)}, bf16[2,16,128,128]{3,2,1,0:T(8,128)(2,1)}, u32[]{:S(2)}, u32[]{:S(2)}) %collective-permute-start) | collective-permute-done | bytes 1048608 | tf_op jit(solution)/shard_map/while/body/eval_jaxpr/ppermute | solution.py:16
  852.1 3.0 convert_select_fusion.5
  861.8 20.0 collective-permute-done
  881.8 3.0 convert_select_fusion.5
  891.5 19.0 collective-permute-done
  910.5 3.0 convert_select_fusion.5
  920.2 18.1 collective-permute-done
  938.4 3.0 convert_select_fusion.5
  948.1 17.2 collective-permute-done
  975.0 17.2 collective-permute-done
  1001.9 17.2 collective-permute-done
  1028.7 17.2 collective-permute-done
  1055.1 48.0 %while.78 = (s32[]{:T(128)}, f32[16,128,128]{2,1,0:T(8,128)S(1)}, f32[4,16,64,128]{3,2,1,0:T(8,128)}, s32[4]{0:T(128)S(1)}, s32[]{:T(128)}, /*index=5*/f32[4,16,...) while((s32[]{:T(128)}, f32[16,128,128]{2,1,0:T(8,128)S(1)}, ...), condition=%wide.region_8.10_spmd.clone, body=%wide.region_7.9_spmd.clone.sunk | while | flops 806690816 | bytes 19451036 | solution.py:100
  1115.3 11.7 collective-permute-done.2
  1128.5 12.3 fusion.115
  1150.9 5.2 broadcast_multiply_fusion
  1161.5 316.2 %custom-call.7 = f32[4,16,1,64,64]{3,4,2,1,0:T(8,128)} custom-call(f32[4,16,1,64,64]{4,3,2,1,0:T(8,128)} %add_bitcast_fusion), custom_call_target="InvertDiagBlocksLowerTriangular" | custom-call | tf_op jit(solution)/shard_map/triangular_solve/custom-call.1 | solution.py:42
  1477.7 6.6 fusion.111
  1487.0 54.6 %while.81 = (s32[]{:T(128)}, f32[16,128,128]{2,1,0:T(8,128)S(1)}, f32[16,128,128]{2,1,0:T(8,128)}, s32[4]{0:T(128)S(1)}, s32[]{:T(128)}, /*index=5*/f32[4,16,64,...) while((s32[]{:T(128)}, f32[16,128,128]{2,1,0:T(8,128)S(1)}, ...), condition=%wide.region_13.15_spmd.clone, body=%wide.region_12.14_spmd.clone.sunk | while | flops 807534592 | bytes 19401408 | solution.py:133
  1497.3 3.1 convolution_subtract_fusion.16
  1511.1 3.1 convolution_subtract_fusion.16
  1524.8 3.1 convolution_subtract_fusion.16
  1538.5 3.1 convolution_subtract_fusion.16
  1541.7 3.6 convert_bitcast_fusion.1
  1545.3 471.8 %while.77 = (s32[]{:T(128)}, f32[2,16,128,128]{3,2,1,0:T(8,128)}, pred[]{:T(512)}, f32[16,128,128]{2,1,0:T(8,128)S(1)}, f32[16,128,128]{2,1,0:T(8,128)}, /*index=5*/f32[2,16,128,128]{3,2,1,0:T(8,128)S(1)}, s32[]{:T(128)}) while((s32[]{:T(128)}, f32[2,16,128,128]{3,2,1,0:T(8,128)}, pred[]{:T(512)}, f32[16,128,128]{2,1,0:T(8,128)S(1)}, ...), condition=%wide.region_15.17_spmd, body=%wide.region_14.16_spmd.sunk | while | flops 807665664 | bytes 22020240 | solution.py:187
  1553.4 26.6 %collective-permute-done.1 = bf16[2,16,128,128]{3,2,1,0:T(8,128)(2,1)} collective-permute-done((bf16[2,16,128,128]{3,2,1,0:T(8,128)(2,1)}, bf16[2,16,128,128]{3,2,1,0:T(8,128)(2,1)}, u32[]{:S(2)}, u32[]{:S(2)}) %collective-permute-start.1) | collective-permute-done | bytes 1048608 | tf_op jit(solution)/shard_map/while/body/eval_jaxpr/ppermute | solution.py:16
  1590.7 25.7 %collective-permute-done.1 = bf16[2,16,128,128]{3,2,1,0:T(8,128)(2,1)} collective-permute-done((bf16[2,16,128,128]{3,2,1,0:T(8,128)(2,1)}, bf16[2,16,128,128]{3,2,1,0:T(8,128)(2,1)}, u32[]{:S(2)}, u32[]{:S(2)}) %collective-permute-start.1) | collective-permute-done | bytes 1048608 | tf_op jit(solution)/shard_map/while/body/eval_jaxpr/ppermute | solution.py:16
  1627.1 24.8 %collective-permute-done.1 = bf16[2,16,128,128]{3,2,1,0:T(8,128)(2,1)} collective-permute-done((bf16[2,16,128,128]{3,2,1,0:T(8,128)(2,1)}, bf16[2,16,128,128]{3,2,1,0:T(8,128)(2,1)}, u32[]{:S(2)}, u32[]{:S(2)}) %collective-permute-start.1) | collective-permute-done | bytes 1048608 | tf_op jit(solution)/shard_map/while/body/eval_jaxpr/ppermute | solution.py:16
  1662.6 23.8 %collective-permute-done.1 = bf16[2,16,128,128]{3,2,1,0:T(8,128)(2,1)} collective-permute-done((bf16[2,16,128,128]{3,2,1,0:T(8,128)(2,1)}, bf16[2,16,128,128]{3,2,1,0:T(8,128)(2,1)}, u32[]{:S(2)}, u32[]{:S(2)}) %collective-permute-start.1) | collective-permute-done | bytes 1048608 | tf_op jit(solution)/shard_map/while/body/eval_jaxpr/ppermute | solution.py:16
  1697.2 22.9 %collective-permute-done.1 = bf16[2,16,128,128]{3,2,1,0:T(8,128)(2,1)} collective-permute-done((bf16[2,16,128,128]{3,2,1,0:T(8,128)(2,1)}, bf16[2,16,128,128]{3,2,1,0:T(8,128)(2,1)}, u32[]{:S(2)}, u32[]{:S(2)}) %collective-permute-start.1) | collective-permute-done | bytes 1048608 | tf_op jit(solution)/shard_map/while/body/eval_jaxpr/ppermute | solution.py:16
  1730.8 22.0 %collective-permute-done.1 = bf16[2,16,128,128]{3,2,1,0:T(8,128)(2,1)} collective-permute-done((bf16[2,16,128,128]{3,2,1,0:T(8,128)(2,1)}, bf16[2,16,128,128]{3,2,1,0:T(8,128)(2,1)}, u32[]{:S(2)}, u32[]{:S(2)}) %collective-permute-start.1) | collective-permute-done | bytes 1048608 | tf_op jit(solution)/shard_map/while/body/eval_jaxpr/ppermute | solution.py:16
  1763.6 21.1 %collective-permute-done.1 = bf16[2,16,128,128]{3,2,1,0:T(8,128)(2,1)} collective-permute-done((bf16[2,16,128,128]{3,2,1,0:T(8,128)(2,1)}, bf16[2,16,128,128]{3,2,1,0:T(8,128)(2,1)}, u32[]{:S(2)}, u32[]{:S(2)}) %collective-permute-start.1) | collective-permute-done | bytes 1048608 | tf_op jit(solution)/shard_map/while/body/eval_jaxpr/ppermute | solution.py:16
  1795.3 20.1 collective-permute-done.1
  1826.2 19.2 collective-permute-done.1
  1856.2 18.3 collective-permute-done.1
  1885.2 17.4 collective-permute-done.1
  1913.3 17.2 collective-permute-done.1
  1941.2 17.2 collective-permute-done.1
  1969.2 17.2 collective-permute-done.1
  1997.1 17.2 collective-permute-done.1
  2021.2 44.4 %while.79 = (s32[]{:T(128)}, f32[16,128,128]{2,1,0:T(8,128)S(1)}, f32[4,16,64,128]{3,2,1,0:T(8,128)}, s32[4]{0:T(128)S(1)}, s32[]{:T(128)}, /*index=5*/f32[4,16,...) while((s32[]{:T(128)}, f32[16,128,128]{2,1,0:T(8,128)S(1)}, ...), condition=%wide.region_19.21_spmd.clone, body=%wide.region_18.20_spmd.clone.sunk | while | flops 806690816 | bytes 12109449 | solution.py:100
  2070.0 3.9 fusion.148
  (437 shorter events, 490.4 us)
Async XLA Ops:
  6.5 1042.4 %copy-start = (f32[1,16,128,128]{3,2,1,0:T(8,128)S(1)}, f32[1,16,128,128]{3,2,1,0:T(8,128)}, u32[]{:S(2)}) copy-start(f32[1,16,128,128]{3,2,1,0:T(8,128)} %param.28) | copy-start | bytes 3145732
  6.5 25.2 %copy-start.17 = (bf16[1,256,2048]{2,1,0:T(8,128)(2,1)S(1)}, bf16[1,256,2048]{2,1,0:T(8,128)(2,1)}, u32[]{:S(2)}) copy-start(bf16[1,256,2048]{2,1,0:T(8,128)(2,1)} %param.22) | copy-start | bytes 3145732
  6.5 25.5 %copy-start.21 = (f32[1,2048]{1,0:T(1,128)S(1)}, f32[1,2048]{1,0:T(1,128)}, u32[]{:S(2)}) copy-start(f32[1,2048]{1,0:T(1,128)} %param.26) | copy-start | bytes 24580
  6.5 25.5 %copy-start.22 = (f32[1,16]{1,0:T(1,128)S(1)}, f32[1,16]{1,0:T(1,128)}, u32[]{:S(2)}) copy-start(f32[1,16]{1,0:T(1,128)} %param.25) | copy-start | bytes 196
  6.5 159.2 %all-gather.4.cloned.1.call-start = ((), (), s32[]{:S(2)}) async-start(), calls=%async_computation.1 | async-start | bytes 26738688 | tf_op jit(solution)/shard_map/all_gather | solution.py:161
  7.3 1538.0 %all-reduce.3.cloned.1.call-start = ((), (), s32[]{:S(2)}) async-start(), calls=%async_computation | async-start | bytes 1048576 | tf_op jit(solution)/shard_map/psum | solution.py:21
  33.0 2.7 copy-start.20
  584.6 2.5 copy-start.9
  589.4 29.2 %collective-permute-start = (bf16[2,16,128,128]{3,2,1,0:T(8,128)(2,1)}, bf16[2,16,128,128]{3,2,1,0:T(8,128)(2,1)}, u32[]{:S(2)}, u32[]{:S(2)}) collective-permute-start(bf16[2,16,128,128]{3,2,1,0:T(8,128)(2,1)} %pad_maximum_fusion.4), channel_id=1, source_target_pairs={{0,1},{1,2},{2,3},{3,4},{4,5},{5,6},{6,7},{7,8},{8,9},{9,10},{10,1... | collective-permute-start | bytes 3145736 | tf_op jit(solution)/shard_map/while/body/eval_jaxpr/ppermute | solution.py:16
  621.6 2.5 copy-start.9
  626.4 28.3 %collective-permute-start = (bf16[2,16,128,128]{3,2,1,0:T(8,128)(2,1)}, bf16[2,16,128,128]{3,2,1,0:T(8,128)(2,1)}, u32[]{:S(2)}, u32[]{:S(2)}) collective-permute-start(bf16[2,16,128,128]{3,2,1,0:T(8,128)(2,1)} %pad_maximum_fusion.4), channel_id=1, source_target_pairs={{0,1},{1,2},{2,3},{3,4},{4,5},{5,6},{6,7},{7,8},{8,9},{9,10},{10,1... | collective-permute-start | bytes 3145736 | tf_op jit(solution)/shard_map/while/body/eval_jaxpr/ppermute | solution.py:16
  657.8 2.5 copy-start.9
  662.6 27.4 %collective-permute-start = (bf16[2,16,128,128]{3,2,1,0:T(8,128)(2,1)}, bf16[2,16,128,128]{3,2,1,0:T(8,128)(2,1)}, u32[]{:S(2)}, u32[]{:S(2)}) collective-permute-start(bf16[2,16,128,128]{3,2,1,0:T(8,128)(2,1)} %pad_maximum_fusion.4), channel_id=1, source_target_pairs={{0,1},{1,2},{2,3},{3,4},{4,5},{5,6},{6,7},{7,8},{8,9},{9,10},{10,1... | collective-permute-start | bytes 3145736 | tf_op jit(solution)/shard_map/while/body/eval_jaxpr/ppermute | solution.py:16
  693.0 2.5 copy-start.9
  697.8 26.5 %collective-permute-start = (bf16[2,16,128,128]{3,2,1,0:T(8,128)(2,1)}, bf16[2,16,128,128]{3,2,1,0:T(8,128)(2,1)}, u32[]{:S(2)}, u32[]{:S(2)}) collective-permute-start(bf16[2,16,128,128]{3,2,1,0:T(8,128)(2,1)} %pad_maximum_fusion.4), channel_id=1, source_target_pairs={{0,1},{1,2},{2,3},{3,4},{4,5},{5,6},{6,7},{7,8},{8,9},{9,10},{10,1... | collective-permute-start | bytes 3145736 | tf_op jit(solution)/shard_map/while/body/eval_jaxpr/ppermute | solution.py:16
  727.2 2.5 copy-start.9
  732.0 25.6 %collective-permute-start = (bf16[2,16,128,128]{3,2,1,0:T(8,128)(2,1)}, bf16[2,16,128,128]{3,2,1,0:T(8,128)(2,1)}, u32[]{:S(2)}, u32[]{:S(2)}) collective-permute-start(bf16[2,16,128,128]{3,2,1,0:T(8,128)(2,1)} %pad_maximum_fusion.4), channel_id=1, source_target_pairs={{0,1},{1,2},{2,3},{3,4},{4,5},{5,6},{6,7},{7,8},{8,9},{9,10},{10,1... | collective-permute-start | bytes 3145736 | tf_op jit(solution)/shard_map/while/body/eval_jaxpr/ppermute | solution.py:16
  760.6 2.5 copy-start.9
  765.4 24.6 %collective-permute-start = (bf16[2,16,128,128]{3,2,1,0:T(8,128)(2,1)}, bf16[2,16,128,128]{3,2,1,0:T(8,128)(2,1)}, u32[]{:S(2)}, u32[]{:S(2)}) collective-permute-start(bf16[2,16,128,128]{3,2,1,0:T(8,128)(2,1)} %pad_maximum_fusion.4), channel_id=1, source_target_pairs={{0,1},{1,2},{2,3},{3,4},{4,5},{5,6},{6,7},{7,8},{8,9},{9,10},{10,1... | collective-permute-start | bytes 3145736 | tf_op jit(solution)/shard_map/while/body/eval_jaxpr/ppermute | solution.py:16
  793.0 2.5 copy-start.9
  797.8 23.7 %collective-permute-start = (bf16[2,16,128,128]{3,2,1,0:T(8,128)(2,1)}, bf16[2,16,128,128]{3,2,1,0:T(8,128)(2,1)}, u32[]{:S(2)}, u32[]{:S(2)}) collective-permute-start(bf16[2,16,128,128]{3,2,1,0:T(8,128)(2,1)} %pad_maximum_fusion.4), channel_id=1, source_target_pairs={{0,1},{1,2},{2,3},{3,4},{4,5},{5,6},{6,7},{7,8},{8,9},{9,10},{10,1... | collective-permute-start | bytes 3145736 | tf_op jit(solution)/shard_map/while/body/eval_jaxpr/ppermute | solution.py:16
  824.5 2.5 copy-start.9
  829.3 22.8 %collective-permute-start = (bf16[2,16,128,128]{3,2,1,0:T(8,128)(2,1)}, bf16[2,16,128,128]{3,2,1,0:T(8,128)(2,1)}, u32[]{:S(2)}, u32[]{:S(2)}) collective-permute-start(bf16[2,16,128,128]{3,2,1,0:T(8,128)(2,1)} %pad_maximum_fusion.4), channel_id=1, source_target_pairs={{0,1},{1,2},{2,3},{3,4},{4,5},{5,6},{6,7},{7,8},{8,9},{9,10},{10,1... | collective-permute-start | bytes 3145736 | tf_op jit(solution)/shard_map/while/body/eval_jaxpr/ppermute | solution.py:16
  855.1 2.5 copy-start.9
  859.9 21.9 %collective-permute-start = (bf16[2,16,128,128]{3,2,1,0:T(8,128)(2,1)}, bf16[2,16,128,128]{3,2,1,0:T(8,128)(2,1)}, u32[]{:S(2)}, u32[]{:S(2)}) collective-permute-start(bf16[2,16,128,128]{3,2,1,0:T(8,128)(2,1)} %pad_maximum_fusion.4), channel_id=1, source_target_pairs={{0,1},{1,2},{2,3},{3,4},{4,5},{5,6},{6,7},{7,8},{8,9},{9,10},{10,1... | collective-permute-start | bytes 3145736 | tf_op jit(solution)/shard_map/while/body/eval_jaxpr/ppermute | solution.py:16
  884.8 2.5 copy-start.9
  889.6 20.9 %collective-permute-start = (bf16[2,16,128,128]{3,2,1,0:T(8,128)(2,1)}, bf16[2,16,128,128]{3,2,1,0:T(8,128)(2,1)}, u32[]{:S(2)}, u32[]{:S(2)}) collective-permute-start(bf16[2,16,128,128]{3,2,1,0:T(8,128)(2,1)} %pad_maximum_fusion.4), channel_id=1, source_target_pairs={{0,1},{1,2},{2,3},{3,4},{4,5},{5,6},{6,7},{7,8},{8,9},{9,10},{10,1... | collective-permute-start | bytes 3145736 | tf_op jit(solution)/shard_map/while/body/eval_jaxpr/ppermute | solution.py:16
  913.5 2.5 copy-start.9
  918.3 20.0 collective-permute-start
  941.3 2.5 copy-start.9
  946.1 19.1 collective-permute-start
  968.2 2.5 copy-start.9
  973.0 19.1 collective-permute-start
  995.1 2.5 copy-start.9
  999.9 19.1 collective-permute-start
  1022.0 2.5 copy-start.9
  1026.8 19.1 collective-permute-start
  1048.9 2.9 copy-start.16
  1103.1 5.5 copy-start.4
  1109.8 2.6 copy-start.3
  1112.5 14.5 collective-permute-start.2
  1502.3 2.7 copy-start.6
  1516.1 2.7 copy-start.6
  1529.8 2.7 copy-start.6
  1545.5 2.5 copy-start.8
  1551.5 28.5 %collective-permute-start.1 = (bf16[2,16,128,128]{3,2,1,0:T(8,128)(2,1)}, bf16[2,16,128,128]{3,2,1,0:T(8,128)(2,1)}, u32[]{:S(2)}, u32[]{:S(2)}) collective-permute-start(bf16[2,16,128,128]{3,2,1,0:T(8,128)(2,1)} %pad_maximum_fusion.5), channel_id=1, source_target_pairs={{0,1},{1,2},{2,3},{3,4},{4,5},{5,6},{6,7},{7,8},{8,9},{9,10},{10,1... | collective-permute-start | bytes 3145736 | tf_op jit(solution)/shard_map/while/body/eval_jaxpr/ppermute | solution.py:16
  1588.8 27.6 %collective-permute-start.1 = (bf16[2,16,128,128]{3,2,1,0:T(8,128)(2,1)}, bf16[2,16,128,128]{3,2,1,0:T(8,128)(2,1)}, u32[]{:S(2)}, u32[]{:S(2)}) collective-permute-start(bf16[2,16,128,128]{3,2,1,0:T(8,128)(2,1)} %pad_maximum_fusion.5), channel_id=1, source_target_pairs={{0,1},{1,2},{2,3},{3,4},{4,5},{5,6},{6,7},{7,8},{8,9},{9,10},{10,1... | collective-permute-start | bytes 3145736 | tf_op jit(solution)/shard_map/while/body/eval_jaxpr/ppermute | solution.py:16
  1625.2 26.7 %collective-permute-start.1 = (bf16[2,16,128,128]{3,2,1,0:T(8,128)(2,1)}, bf16[2,16,128,128]{3,2,1,0:T(8,128)(2,1)}, u32[]{:S(2)}, u32[]{:S(2)}) collective-permute-start(bf16[2,16,128,128]{3,2,1,0:T(8,128)(2,1)} %pad_maximum_fusion.5), channel_id=1, source_target_pairs={{0,1},{1,2},{2,3},{3,4},{4,5},{5,6},{6,7},{7,8},{8,9},{9,10},{10,1... | collective-permute-start | bytes 3145736 | tf_op jit(solution)/shard_map/while/body/eval_jaxpr/ppermute | solution.py:16
  1660.7 25.8 %collective-permute-start.1 = (bf16[2,16,128,128]{3,2,1,0:T(8,128)(2,1)}, bf16[2,16,128,128]{3,2,1,0:T(8,128)(2,1)}, u32[]{:S(2)}, u32[]{:S(2)}) collective-permute-start(bf16[2,16,128,128]{3,2,1,0:T(8,128)(2,1)} %pad_maximum_fusion.5), channel_id=1, source_target_pairs={{0,1},{1,2},{2,3},{3,4},{4,5},{5,6},{6,7},{7,8},{8,9},{9,10},{10,1... | collective-permute-start | bytes 3145736 | tf_op jit(solution)/shard_map/while/body/eval_jaxpr/ppermute | solution.py:16
  1689.3 2.5 copy-start.8
  1695.3 24.8 %collective-permute-start.1 = (bf16[2,16,128,128]{3,2,1,0:T(8,128)(2,1)}, bf16[2,16,128,128]{3,2,1,0:T(8,128)(2,1)}, u32[]{:S(2)}, u32[]{:S(2)}) collective-permute-start(bf16[2,16,128,128]{3,2,1,0:T(8,128)(2,1)} %pad_maximum_fusion.5), channel_id=1, source_target_pairs={{0,1},{1,2},{2,3},{3,4},{4,5},{5,6},{6,7},{7,8},{8,9},{9,10},{10,1... | collective-permute-start | bytes 3145736 | tf_op jit(solution)/shard_map/while/body/eval_jaxpr/ppermute | solution.py:16
  1728.9 23.9 %collective-permute-start.1 = (bf16[2,16,128,128]{3,2,1,0:T(8,128)(2,1)}, bf16[2,16,128,128]{3,2,1,0:T(8,128)(2,1)}, u32[]{:S(2)}, u32[]{:S(2)}) collective-permute-start(bf16[2,16,128,128]{3,2,1,0:T(8,128)(2,1)} %pad_maximum_fusion.5), channel_id=1, source_target_pairs={{0,1},{1,2},{2,3},{3,4},{4,5},{5,6},{6,7},{7,8},{8,9},{9,10},{10,1... | collective-permute-start | bytes 3145736 | tf_op jit(solution)/shard_map/while/body/eval_jaxpr/ppermute | solution.py:16
  1761.6 23.0 %collective-permute-start.1 = (bf16[2,16,128,128]{3,2,1,0:T(8,128)(2,1)}, bf16[2,16,128,128]{3,2,1,0:T(8,128)(2,1)}, u32[]{:S(2)}, u32[]{:S(2)}) collective-permute-start(bf16[2,16,128,128]{3,2,1,0:T(8,128)(2,1)} %pad_maximum_fusion.5), channel_id=1, source_target_pairs={{0,1},{1,2},{2,3},{3,4},{4,5},{5,6},{6,7},{7,8},{8,9},{9,10},{10,1... | collective-permute-start | bytes 3145736 | tf_op jit(solution)/shard_map/while/body/eval_jaxpr/ppermute | solution.py:16
  1793.4 22.1 %collective-permute-start.1 = (bf16[2,16,128,128]{3,2,1,0:T(8,128)(2,1)}, bf16[2,16,128,128]{3,2,1,0:T(8,128)(2,1)}, u32[]{:S(2)}, u32[]{:S(2)}) collective-permute-start(bf16[2,16,128,128]{3,2,1,0:T(8,128)(2,1)} %pad_maximum_fusion.5), channel_id=1, source_target_pairs={{0,1},{1,2},{2,3},{3,4},{4,5},{5,6},{6,7},{7,8},{8,9},{9,10},{10,1... | collective-permute-start | bytes 3145736 | tf_op jit(solution)/shard_map/while/body/eval_jaxpr/ppermute | solution.py:16
  1824.3 21.1 %collective-permute-start.1 = (bf16[2,16,128,128]{3,2,1,0:T(8,128)(2,1)}, bf16[2,16,128,128]{3,2,1,0:T(8,128)(2,1)}, u32[]{:S(2)}, u32[]{:S(2)}) collective-permute-start(bf16[2,16,128,128]{3,2,1,0:T(8,128)(2,1)} %pad_maximum_fusion.5), channel_id=1, source_target_pairs={{0,1},{1,2},{2,3},{3,4},{4,5},{5,6},{6,7},{7,8},{8,9},{9,10},{10,1... | collective-permute-start | bytes 3145736 | tf_op jit(solution)/shard_map/while/body/eval_jaxpr/ppermute | solution.py:16
  1854.3 20.2 collective-permute-start.1
  1883.3 19.3 collective-permute-start.1
  1911.4 19.1 collective-permute-start.1
  1939.3 19.1 collective-permute-start.1
  1967.2 19.1 collective-permute-start.1
  1995.2 19.1 collective-permute-start.1
  2017.1 4.1 copy-start.10
  2065.6 2.5 copy-start.13
  2070.0 3.9 copy-start.1
  (32 other events, 69.1 us)
Sparse Core Ops, SparseCore 0:
  9.5 156.2 all-gather.3
  1115.4 85.1 all-reduce.2
where the time goes:
time: 2100 us; the launch traced here: 2080 us
  other arithmetic  789 us (38%)
  waiting for transfers between devices  771 us (37%)
  matrix products  326 us (16%)
  local copies, waits for them, and re-layouts  74.7 us (4%)
  starting transfers between devices  57.7 us (3%)
  blocking collectives  24.4 us (1%)
  loops' own time  23.7 us (1%)
    another operation x5, other arithmetic, block_solve(): lax.linalg.triangular_solve(system, right_side, left_side=True, lower=Tru...  632 us
    ppermute x30, waiting for transfers between devices, from_behind(): return lax.ppermute(value, axis, pairs)  629 us
    all_gather x1, waiting for transfers between devices, shards(): lax.all_gather(w_qkv[0], 'seq', axis=0, tiled=True)  130 us
    select_n x30, other arithmetic, hop_once(): return jnp.where(position == 0, empty_map, passed)  87.6 us
    dot_general x30, matrix products, compose(): jnp.einsum('hij,hjk->hik', latter[0], earlier[0], precision=FULL_PRECISION)  74.3 us
    ppermute x30, starting transfers between devices, from_behind(): return lax.ppermute(value, axis, pairs)  57.6 us
    dot_general x30, matrix products, compose(): jnp.einsum('hij,hjk->hik', latter[0], earlier[1], precision=FULL_PRECISION)  54.3 us
  transfers between devices with their start and end apart: 33, of which 32 were waited for; matrix products, arithmetic and copies ran while one was open for 20% of the time, Pallas kernels for 0%

commit v1 on v0

--- a/solution.py
+++ b/solution.py
@@ -8,6 +8,28 @@
 GROUP = 64
 TICKS = 2
 FULL_PRECISION = lax.Precision.HIGHEST
+
+
+def in_order(blocks, dim):
+    blocks = jnp.moveaxis(blocks, 0, dim)
+    shape = blocks.shape
+    return blocks.reshape(*shape[:dim], shape[dim] * shape[dim + 1], *shape[dim + 2 :])
+
+
+def collect(shard, axis, dim):
+    size = lax.axis_size(axis)
+    pairs = [(i, (i + 1) % size) for i in range(size)]
+    back = [(b, a) for a, b in pairs]
+    lower, upper = ([], [])
+    for turn in range(size - 1):
+        if turn % 2 == 0:
+            lower.append(lax.ppermute(lower[-1] if lower else shard, axis, pairs))
+        else:
+            upper.append(lax.ppermute(upper[-1] if upper else shard, axis, back))
+    blocks = jnp.stack([*lower[::-1], shard, *upper])
+    shift = lax.axis_index(axis) - len(lower)
+    blocks = blocks[(jnp.arange(size) - shift) % size]
+    return in_order(blocks, dim)
 
 
 def from_behind(value, axis, by):
@@ -158,7 +180,7 @@
 
 def shards(residual, w_qkv, w_beta, beta_bias, norm_gain, out_gain, state_in, doc_start):
     weight_qkv, weight_beta = (
-        lax.all_gather(w_qkv[0], "seq", axis=0, tiled=True),
+        collect(w_qkv[0], "seq", 0),
         lax.all_gather(w_beta[0], "seq", axis=0, tiled=True),
     )
     seq_count = lax.axis_size("seq")

time: 2100 us -> 2300 us (1.095)
  waiting for transfers between devices: 771 us -> 863 us
  local copies, waits for them, and re-layouts: 74.7 us -> 122 us
  blocking collectives: 24.4 us -> 54.6 us
  starting transfers between devices: 57.7 us -> 87.3 us
    ppermute x0 -> x15, waiting for transfers between devices: none -> 221 us  [the longest x8 220 us: collect(): lower.append(lax.ppermute(lower[-1] if lower else shard, axis, pairs))]
    all_gather x1 -> x0, waiting for transfers between devices: 130 us -> none  [shards(): lax.all_gather(w_qkv[0], 'seq', axis=0, tiled=True)]
    unnamed x38 -> x87, local copies, waits for them, and re-layouts: 8.31 us -> 39 us
    all_gather x1, blocking collectives: 24.4 us -> 54.6 us  [shards(): lax.all_gather(w_beta[0], 'seq', axis=0, tiled=True)]
    ppermute x0 -> x15, starting transfers between devices: none -> 30 us  [the longest x7 28.4 us: collect(): upper.append(lax.ppermute(upper[-1] if upper else shard, axis, back))]
  transfers between devices with their start and end apart: 33 -> 47, of which waited for: 32 -> 41; matrix products, arithmetic and copies ran while one was open for 20% -> 19% of each run, Pallas kernels for 0% -> 0%
where the time goes in v1:
time: 2300 us; the launch traced here: 2280 us
  waiting for transfers between devices  863 us (38%)
  other arithmetic  788 us (34%)
  matrix products  326 us (14%)
  local copies, waits for them, and re-layouts  122 us (5%)
  starting transfers between devices  87.3 us (4%)
  blocking collectives  54.6 us (2%)
    another operation x5, other arithmetic, block_solve(): lax.linalg.triangular_solve(system, right_side, left_side=True, lower=Tru...  632 us
    ppermute x30, waiting for transfers between devices, from_behind(): return lax.ppermute(value, axis, pairs)  630 us
    ppermute x8, waiting for transfers between devices, collect(): lower.append(lax.ppermute(lower[-1] if lower else shard, axis, pairs))  220 us
    select_n x30, other arithmetic, hop_once(): return jnp.where(position == 0, empty_map, passed)  86.3 us
    dot_general x30, matrix products, compose(): jnp.einsum('hij,hjk->hik', latter[0], earlier[0], precision=FULL_PRECISION)  74.3 us
    ppermute x30, starting transfers between devices, from_behind(): return lax.ppermute(value, axis, pairs)  57.3 us
    all_gather x1, blocking collectives, shards(): lax.all_gather(w_beta[0], 'seq', axis=0, tiled=True)  54.6 us
    dot_general x30, matrix products, compose(): jnp.einsum('hij,hjk->hik', latter[0], earlier[1], precision=FULL_PRECISION)  54.3 us
  transfers between devices with their start and end apart: 47, of which 41 were waited for; matrix products, arithmetic and copies ran while one was open for 19% of the time, Pallas kernels for 0%

profile of v1, /device:TPU:34, one launch (start us, length us, event | category | flops | bytes accessed | tf_op | source)
XLA Modules:
  0.0 2278.6 jit_solution(1218036770422288263)
XLA Ops:
  8.1 36.9 %collective-permute-done.2 = bf16[128,6144]{1,0:T(8,128)(2,1)S(1)} collective-permute-done((bf16[128,6144]{1,0:T(8,128)(2,1)}, bf16[128,6144]{1,0:T(8,128)(2,1)S(1)}, u32[]{:S(2)}, u32[]{:S(2)}) %collective-permute-start.2) | collective-permute-done | bytes 1572896 | tf_op jit(solution)/shard_map/ppermute | solution.py:26
  46.1 4.1 collective-permute-start.10
  50.3 33.2 %collective-permute-done.3 = bf16[128,6144]{1,0:T(8,128)(2,1)S(1)} collective-permute-done((bf16[128,6144]{1,0:T(8,128)(2,1)S(1)}, bf16[128,6144]{1,0:T(8,128)(2,1)S(1)}, u32[]{:S(2)}, u32[]{:S(2)}) %collective-permute-start.3) | collective-permute-done | bytes 1572896 | tf_op jit(solution)/shard_map/ppermute | solution.py:26
  84.7 4.1 collective-permute-start.11
  88.8 31.2 %collective-permute-done.4 = bf16[128,6144]{1,0:T(8,128)(2,1)S(1)} collective-permute-done((bf16[128,6144]{1,0:T(8,128)(2,1)S(1)}, bf16[128,6144]{1,0:T(8,128)(2,1)S(1)}, u32[]{:S(2)}, u32[]{:S(2)}) %collective-permute-start.4) | collective-permute-done | bytes 1572896 | tf_op jit(solution)/shard_map/ppermute | solution.py:26
  120.4 4.6 collective-permute-start.12
  125.0 30.5 %collective-permute-done.5 = bf16[128,6144]{1,0:T(8,128)(2,1)S(1)} collective-permute-done((bf16[128,6144]{1,0:T(8,128)(2,1)S(1)}, bf16[128,6144]{1,0:T(8,128)(2,1)S(1)}, u32[]{:S(2)}, u32[]{:S(2)}) %collective-permute-start.5) | collective-permute-done | bytes 1572896 | tf_op jit(solution)/shard_map/ppermute | solution.py:26
  155.6 4.6 collective-permute-start.13
  160.2 29.9 %collective-permute-done.6 = bf16[128,6144]{1,0:T(8,128)(2,1)S(1)} collective-permute-done((bf16[128,6144]{1,0:T(8,128)(2,1)S(1)}, bf16[128,6144]{1,0:T(8,128)(2,1)S(1)}, u32[]{:S(2)}, u32[]{:S(2)}) %collective-permute-start.6) | collective-permute-done | bytes 1572896 | tf_op jit(solution)/shard_map/ppermute | solution.py:26
  190.2 4.6 collective-permute-start.14
  194.8 29.9 %collective-permute-done.7 = bf16[128,6144]{1,0:T(8,128)(2,1)S(1)} collective-permute-done((bf16[128,6144]{1,0:T(8,128)(2,1)S(1)}, bf16[128,6144]{1,0:T(8,128)(2,1)S(1)}, u32[]{:S(2)}, u32[]{:S(2)}) %collective-permute-start.7) | collective-permute-done | bytes 1572896 | tf_op jit(solution)/shard_map/ppermute | solution.py:26
  226.7 3.6 collective-permute-start.15
  230.4 28.6 %collective-permute-done.8 = bf16[128,6144]{1,0:T(8,128)(2,1)} collective-permute-done((bf16[128,6144]{1,0:T(8,128)(2,1)S(1)}, bf16[128,6144]{1,0:T(8,128)(2,1)}, u32[]{:S(2)}, u32[]{:S(2)}) %collective-permute-start.8) | collective-permute-done | bytes 1572896 | tf_op jit(solution)/shard_map/ppermute | solution.py:26
  259.1 54.6 %all-gather = bf16[1,2048,16]{1,2,0:T(8,128)(2,1)S(1)} all-gather(bf16[1,128,16]{1,2,0:T(8,128)(2,1)} %param.24), channel_id=2, replica_groups=mesh['section'=8,'seq'=16] {'seq'}, dimensions={1}, use_global_device_ids=true | all-gather | bytes 69632 | tf_op jit(solution)/shard_map/all_gather | solution.py:184
  354.7 18.7 gather_fusion
  373.4 32.9 %copy.59 = bf16[6144,2048]{1,0:T(8,128)(2,1)} copy(bf16[6144,2048]{0,1:T(8,128)(2,1)} %bitcast.384) | data formatting | bytes 50331648 | tf_op jit(solution)/shard_map/dot_general | solution.py:77
  406.3 11.4 fusion.151
  420.6 3.9 broadcast_multiply_fusion.1
  428.6 316.0 %custom-call.6 = f32[4,16,1,64,64]{3,4,2,1,0:T(8,128)} custom-call(f32[4,16,1,64,64]{4,3,2,1,0:T(8,128)} %add_bitcast_fusion.1), custom_call_target="InvertDiagBlocksLowerTriangular" | custom-call | tf_op jit(solution)/shard_map/triangular_solve/custom-call.1 | solution.py:64
  744.5 6.6 fusion.110
  753.9 41.5 %while.80 = (s32[]{:T(128)}, f32[16,128,128]{2,1,0:T(8,128)S(1)}, f32[16,128,128]{2,1,0:T(8,128)S(1)}, s32[4]{0:T(128)S(1)}, s32[]{:T(128)}, /*index=5*/f32[4,16...) while((s32[]{:T(128)}, f32[16,128,128]{2,1,0:T(8,128)S(1)}, ...), condition=%wide.region_3.5_spmd.clone, body=%wide.region_2.4_spmd.clone.sunk | while | flops 807534592 | bytes 19400364 | solution.py:155
  798.4 465.0 %while.76 = (s32[]{:T(128)}, f32[2,16,128,128]{3,2,1,0:T(8,128)}, pred[]{:T(512)}, f32[16,128,128]{2,1,0:T(8,128)S(1)}, f32[16,128,128]{2,1,0:T(8,128)S(1)}, /*index=5*/f32[2,16,128,128]{3,2,1,0:T(8,128)}, s32[]{:T(128)}) while((s32[]{:T(128)}, f32[2,16,128,128]{3,2,1,0:T(8,128)}, pred[]{:T(512)}, f32[16,128,128]{2,1,0:T(8,128)S(1)}, ...), condition=%wide.region_5.7_spmd, body=%wide.region_4.6_spmd.sunk | while | flops 807665664 | bytes 26214544 | solution.py:209
  805.1 17.2 collective-permute-done
  832.0 17.2 collective-permute-done
  858.8 17.2 collective-permute-done
  885.7 17.4 collective-permute-done
  912.8 18.5 collective-permute-done
  941.0 19.6 collective-permute-done
  970.2 20.6 collective-permute-done
  1000.5 21.7 collective-permute-done
  1031.9 22.8 %collective-permute-done = bf16[2,16,128,128]{3,2,1,0:T(8,128)(2,1)} collective-permute-done((bf16[2,16,128,128]{3,2,1,0:T(8,128)(2,1)}, bf16[2,16,128,128]{3,2,1,0:T(8,128)(2,1)}, u32[]{:S(2)}, u32[]{:S(2)}) %collective-permute-start) | collective-permute-done | bytes 1048608 | tf_op jit(solution)/shard_map/while/body/eval_jaxpr/ppermute | solution.py:38
  1064.4 23.9 %collective-permute-done = bf16[2,16,128,128]{3,2,1,0:T(8,128)(2,1)} collective-permute-done((bf16[2,16,128,128]{3,2,1,0:T(8,128)(2,1)}, bf16[2,16,128,128]{3,2,1,0:T(8,128)(2,1)}, u32[]{:S(2)}, u32[]{:S(2)}) %collective-permute-start) | collective-permute-done | bytes 1048608 | tf_op jit(solution)/shard_map/while/body/eval_jaxpr/ppermute | solution.py:38
  1098.0 25.0 %collective-permute-done = bf16[2,16,128,128]{3,2,1,0:T(8,128)(2,1)} collective-permute-done((bf16[2,16,128,128]{3,2,1,0:T(8,128)(2,1)}, bf16[2,16,128,128]{3,2,1,0:T(8,128)(2,1)}, u32[]{:S(2)}, u32[]{:S(2)}) %collective-permute-start) | collective-permute-done | bytes 1048608 | tf_op jit(solution)/shard_map/while/body/eval_jaxpr/ppermute | solution.py:38
  1132.7 26.0 %collective-permute-done = bf16[2,16,128,128]{3,2,1,0:T(8,128)(2,1)} collective-permute-done((bf16[2,16,128,128]{3,2,1,0:T(8,128)(2,1)}, bf16[2,16,128,128]{3,2,1,0:T(8,128)(2,1)}, u32[]{:S(2)}, u32[]{:S(2)}) %collective-permute-start) | collective-permute-done | bytes 1048608 | tf_op jit(solution)/shard_map/while/body/eval_jaxpr/ppermute | solution.py:38
  1168.4 27.2 %collective-permute-done = bf16[2,16,128,128]{3,2,1,0:T(8,128)(2,1)} collective-permute-done((bf16[2,16,128,128]{3,2,1,0:T(8,128)(2,1)}, bf16[2,16,128,128]{3,2,1,0:T(8,128)(2,1)}, u32[]{:S(2)}, u32[]{:S(2)}) %collective-permute-start) | collective-permute-done | bytes 1048608 | tf_op jit(solution)/shard_map/while/body/eval_jaxpr/ppermute | solution.py:38
  1205.2 28.3 %collective-permute-done = bf16[2,16,128,128]{3,2,1,0:T(8,128)(2,1)} collective-permute-done((bf16[2,16,128,128]{3,2,1,0:T(8,128)(2,1)}, bf16[2,16,128,128]{3,2,1,0:T(8,128)(2,1)}, u32[]{:S(2)}, u32[]{:S(2)}) %collective-permute-start) | collective-permute-done | bytes 1048608 | tf_op jit(solution)/shard_map/while/body/eval_jaxpr/ppermute | solution.py:38
  1243.2 17.2 collective-permute-done
  1267.7 47.7 %while.78 = (s32[]{:T(128)}, f32[16,128,128]{2,1,0:T(8,128)S(1)}, f32[4,16,64,128]{3,2,1,0:T(8,128)}, s32[4]{0:T(128)S(1)}, s32[]{:T(128)}, /*index=5*/f32[4,16,...) while((s32[]{:T(128)}, f32[16,128,128]{2,1,0:T(8,128)S(1)}, ...), condition=%wide.region_8.10_spmd.clone, body=%wide.region_7.9_spmd.clone.sunk | while | flops 806690816 | bytes 19451036 | solution.py:122
  1327.6 11.7 collective-permute-done.17
  1340.9 12.1 fusion.154
  1358.6 4.0 broadcast_multiply_fusion
  1366.6 316.0 %custom-call.7 = f32[4,16,1,64,64]{3,4,2,1,0:T(8,128)} custom-call(f32[4,16,1,64,64]{4,3,2,1,0:T(8,128)} %add_bitcast_fusion), custom_call_target="InvertDiagBlocksLowerTriangular" | custom-call | tf_op jit(solution)/shard_map/triangular_solve/custom-call.1 | solution.py:64
  1682.6 6.6 fusion.114
  1691.9 54.5 %while.81 = (s32[]{:T(128)}, f32[16,128,128]{2,1,0:T(8,128)S(1)}, f32[16,128,128]{2,1,0:T(8,128)}, s32[4]{0:T(128)S(1)}, s32[]{:T(128)}, /*index=5*/f32[4,16,64,...) while((s32[]{:T(128)}, f32[16,128,128]{2,1,0:T(8,128)S(1)}, ...), condition=%wide.region_13.15_spmd.clone, body=%wide.region_12.14_spmd.clone.sunk | while | flops 807534592 | bytes 19401408 | solution.py:155
  1702.3 3.1 convolution_subtract_fusion.16
  1715.9 3.1 convolution_subtract_fusion.16
  1749.4 470.7 %while.77 = (s32[]{:T(128)}, f32[2,16,128,128]{3,2,1,0:T(8,128)}, pred[]{:T(512)}, f32[16,128,128]{2,1,0:T(8,128)S(1)}, f32[16,128,128]{2,1,0:T(8,128)}, /*index=5*/f32[2,16,128,128]{3,2,1,0:T(8,128)S(1)}, s32[]{:T(128)}) while((s32[]{:T(128)}, f32[2,16,128,128]{3,2,1,0:T(8,128)}, pred[]{:T(512)}, f32[16,128,128]{2,1,0:T(8,128)S(1)}, ...), condition=%wide.region_15.17_spmd, body=%wide.region_14.16_spmd.sunk | while | flops 807665664 | bytes 22020240 | solution.py:209
  1757.3 26.6 %collective-permute-done.1 = bf16[2,16,128,128]{3,2,1,0:T(8,128)(2,1)} collective-permute-done((bf16[2,16,128,128]{3,2,1,0:T(8,128)(2,1)}, bf16[2,16,128,128]{3,2,1,0:T(8,128)(2,1)}, u32[]{:S(2)}, u32[]{:S(2)}) %collective-permute-start.1) | collective-permute-done | bytes 1048608 | tf_op jit(solution)/shard_map/while/body/eval_jaxpr/ppermute | solution.py:38
  1794.5 25.7 %collective-permute-done.1 = bf16[2,16,128,128]{3,2,1,0:T(8,128)(2,1)} collective-permute-done((bf16[2,16,128,128]{3,2,1,0:T(8,128)(2,1)}, bf16[2,16,128,128]{3,2,1,0:T(8,128)(2,1)}, u32[]{:S(2)}, u32[]{:S(2)}) %collective-permute-start.1) | collective-permute-done | bytes 1048608 | tf_op jit(solution)/shard_map/while/body/eval_jaxpr/ppermute | solution.py:38
  1830.9 24.8 %collective-permute-done.1 = bf16[2,16,128,128]{3,2,1,0:T(8,128)(2,1)} collective-permute-done((bf16[2,16,128,128]{3,2,1,0:T(8,128)(2,1)}, bf16[2,16,128,128]{3,2,1,0:T(8,128)(2,1)}, u32[]{:S(2)}, u32[]{:S(2)}) %collective-permute-start.1) | collective-permute-done | bytes 1048608 | tf_op jit(solution)/shard_map/while/body/eval_jaxpr/ppermute | solution.py:38
  1866.3 23.8 %collective-permute-done.1 = bf16[2,16,128,128]{3,2,1,0:T(8,128)(2,1)} collective-permute-done((bf16[2,16,128,128]{3,2,1,0:T(8,128)(2,1)}, bf16[2,16,128,128]{3,2,1,0:T(8,128)(2,1)}, u32[]{:S(2)}, u32[]{:S(2)}) %collective-permute-start.1) | collective-permute-done | bytes 1048608 | tf_op jit(solution)/shard_map/while/body/eval_jaxpr/ppermute | solution.py:38
  1900.8 22.9 %collective-permute-done.1 = bf16[2,16,128,128]{3,2,1,0:T(8,128)(2,1)} collective-permute-done((bf16[2,16,128,128]{3,2,1,0:T(8,128)(2,1)}, bf16[2,16,128,128]{3,2,1,0:T(8,128)(2,1)}, u32[]{:S(2)}, u32[]{:S(2)}) %collective-permute-start.1) | collective-permute-done | bytes 1048608 | tf_op jit(solution)/shard_map/while/body/eval_jaxpr/ppermute | solution.py:38
  1934.4 22.0 collective-permute-done.1
  1967.1 21.1 collective-permute-done.1
  1998.8 20.1 collective-permute-done.1
  2029.6 19.2 collective-permute-done.1
  2059.5 18.3 collective-permute-done.1
  2088.5 17.4 collective-permute-done.1
  2116.5 17.2 collective-permute-done.1
  2144.4 17.2 collective-permute-done.1
  2172.2 17.2 collective-permute-done.1
  2200.1 17.2 collective-permute-done.1
  2224.1 39.2 %while.79 = (s32[]{:T(128)}, f32[16,128,128]{2,1,0:T(8,128)S(1)}, f32[4,16,64,128]{3,2,1,0:T(8,128)}, s32[4]{0:T(128)S(1)}, s32[]{:T(128)}, /*index=5*/f32[4,16,...) while((s32[]{:T(128)}, f32[16,128,128]{2,1,0:T(8,128)S(1)}, ...), condition=%wide.region_19.21_spmd.clone, body=%wide.region_18.20_spmd.clone.sunk | while | flops 806690816 | bytes 19451036 | solution.py:122
  2267.7 3.9 fusion.149
  (517 shorter events, 561.1 us)
Async XLA Ops:
  6.5 1256.9 %copy-start = (f32[1,16,128,128]{3,2,1,0:T(8,128)S(1)}, f32[1,16,128,128]{3,2,1,0:T(8,128)}, u32[]{:S(2)}) copy-start(f32[1,16,128,128]{3,2,1,0:T(8,128)} %param.28) | copy-start | bytes 3145732
  6.5 1742.9 %all-reduce.3.cloned.1.call-start = ((), (), s32[]{:S(2)}) async-start(), calls=%async_computation | async-start | bytes 1048576 | tf_op jit(solution)/shard_map/psum | solution.py:43
  6.5 38.5 %collective-permute-start.2 = (bf16[128,6144]{1,0:T(8,128)(2,1)}, bf16[128,6144]{1,0:T(8,128)(2,1)S(1)}, u32[]{:S(2)}, u32[]{:S(2)}) collective-permute-start(bf16[128,6144]{1,0:T(8,128)(2,1)} %bitcast.399), channel_id=1, source_target_pairs={{0,1},{1,2},{2,3},{3,4},{4,5},{5,6},{6,7},{7,8},{8,9},{9,10},{10,1... | collective-permute-start | bytes 4718600 | tf_op jit(solution)/shard_map/ppermute | solution.py:26
  46.1 37.4 %collective-permute-start.3 = (bf16[128,6144]{1,0:T(8,128)(2,1)S(1)}, bf16[128,6144]{1,0:T(8,128)(2,1)S(1)}, u32[]{:S(2)}, u32[]{:S(2)}) collective-permute-start(bf16[128,6144]{1,0:T(8,128)(2,1)S(1)} %collective-permute-done.2), channel_id=1, source_target_pairs={{0,1},{1,2},{2,3},{3,4},{4,5},{5,6},{6,7},{7,8},{8,9},{9,10},{10,1... | collective-permute-start | bytes 4718600 | tf_op jit(solution)/shard_map/ppermute | solution.py:26
  46.1 37.4 %collective-permute-start.10 = (bf16[128,6144]{1,0:T(8,128)(2,1)}, bf16[128,6144]{1,0:T(8,128)(2,1)S(1)}, u32[]{:S(2)}, u32[]{:S(2)}) collective-permute-start(bf16[128,6144]{1,0:T(8,128)(2,1)} %bitcast.400), channel_id=1, source_target_pairs={{1,0},{2,1},{3,2},{4,3},{5,4},{6,5},{7,6},{8,7},{9,8},{10,9},{11,1... | collective-permute-start | bytes 4718600 | tf_op jit(solution)/shard_map/ppermute | solution.py:28
  83.5 36.9 %copy-start.22 = (bf16[128,6144]{1,0:T(8,128)(2,1)}, bf16[128,6144]{1,0:T(8,128)(2,1)S(1)}, u32[]{:S(2)}) copy-start(bf16[128,6144]{1,0:T(8,128)(2,1)S(1)} %collective-permute-done.3) | copy-start | bytes 4718596
  83.5 36.5 %collective-permute-start.4 = (bf16[128,6144]{1,0:T(8,128)(2,1)S(1)}, bf16[128,6144]{1,0:T(8,128)(2,1)S(1)}, u32[]{:S(2)}, u32[]{:S(2)}) collective-permute-start(bf16[128,6144]{1,0:T(8,128)(2,1)S(1)} %collective-permute-done.3), channel_id=1, source_target_pairs={{0,1},{1,2},{2,3},{3,4},{4,5},{5,6},{6,7},{7,8},{8,9},{9,10},{10,1... | collective-permute-start | bytes 4718600 | tf_op jit(solution)/shard_map/ppermute | solution.py:26
  84.7 35.7 %collective-permute-start.11 = (bf16[128,6144]{1,0:T(8,128)(2,1)S(1)}, bf16[128,6144]{1,0:T(8,128)(2,1)S(1)}, u32[]{:S(2)}, u32[]{:S(2)}) collective-permute-start(bf16[128,6144]{1,0:T(8,128)(2,1)S(1)} %collective-permute-done.10), channel_id=1, source_target_pairs={{1,0},{2,1},{3,2},{4,3},{5,4},{6,5},{7,6},{8,7},{9,8},{10,9},{11,1... | collective-permute-start | bytes 4718600 | tf_op jit(solution)/shard_map/ppermute | solution.py:28
  120.0 35.7 %copy-start.26 = (bf16[128,6144]{1,0:T(8,128)(2,1)}, bf16[128,6144]{1,0:T(8,128)(2,1)S(1)}, u32[]{:S(2)}) copy-start(bf16[128,6144]{1,0:T(8,128)(2,1)S(1)} %collective-permute-done.4) | copy-start | bytes 4718596
  120.0 35.5 %collective-permute-start.5 = (bf16[128,6144]{1,0:T(8,128)(2,1)S(1)}, bf16[128,6144]{1,0:T(8,128)(2,1)S(1)}, u32[]{:S(2)}, u32[]{:S(2)}) collective-permute-start(bf16[128,6144]{1,0:T(8,128)(2,1)S(1)} %collective-permute-done.4), channel_id=1, source_target_pairs={{0,1},{1,2},{2,3},{3,4},{4,5},{5,6},{6,7},{7,8},{8,9},{9,10},{10,1... | collective-permute-start | bytes 4718600 | tf_op jit(solution)/shard_map/ppermute | solution.py:26
  120.4 4.6 copy-start.24
  120.4 35.2 %collective-permute-start.12 = (bf16[128,6144]{1,0:T(8,128)(2,1)S(1)}, bf16[128,6144]{1,0:T(8,128)(2,1)S(1)}, u32[]{:S(2)}, u32[]{:S(2)}) collective-permute-start(bf16[128,6144]{1,0:T(8,128)(2,1)S(1)} %collective-permute-done.11), channel_id=1, source_target_pairs={{1,0},{2,1},{3,2},{4,3},{5,4},{6,5},{7,6},{8,7},{9,8},{10,9},{11,1... | collective-permute-start | bytes 4718600 | tf_op jit(solution)/shard_map/ppermute | solution.py:28
  155.5 34.7 %copy-start.32 = (bf16[128,6144]{1,0:T(8,128)(2,1)}, bf16[128,6144]{1,0:T(8,128)(2,1)S(1)}, u32[]{:S(2)}) copy-start(bf16[128,6144]{1,0:T(8,128)(2,1)S(1)} %collective-permute-done.5) | copy-start | bytes 4718596
  155.5 34.6 %collective-permute-start.6 = (bf16[128,6144]{1,0:T(8,128)(2,1)S(1)}, bf16[128,6144]{1,0:T(8,128)(2,1)S(1)}, u32[]{:S(2)}, u32[]{:S(2)}) collective-permute-start(bf16[128,6144]{1,0:T(8,128)(2,1)S(1)} %collective-permute-done.5), channel_id=1, source_target_pairs={{0,1},{1,2},{2,3},{3,4},{4,5},{5,6},{6,7},{7,8},{8,9},{9,10},{10,1... | collective-permute-start | bytes 4718600 | tf_op jit(solution)/shard_map/ppermute | solution.py:26
  155.6 4.6 copy-start.28
  155.6 34.6 %collective-permute-start.13 = (bf16[128,6144]{1,0:T(8,128)(2,1)S(1)}, bf16[128,6144]{1,0:T(8,128)(2,1)S(1)}, u32[]{:S(2)}, u32[]{:S(2)}) collective-permute-start(bf16[128,6144]{1,0:T(8,128)(2,1)S(1)} %collective-permute-done.12), channel_id=1, source_target_pairs={{1,0},{2,1},{3,2},{4,3},{5,4},{6,5},{7,6},{8,7},{9,8},{10,9},{11,1... | collective-permute-start | bytes 4718600 | tf_op jit(solution)/shard_map/ppermute | solution.py:28
  190.1 4.7 copy-start.34
  190.1 34.6 %collective-permute-start.7 = (bf16[128,6144]{1,0:T(8,128)(2,1)S(1)}, bf16[128,6144]{1,0:T(8,128)(2,1)S(1)}, u32[]{:S(2)}, u32[]{:S(2)}) collective-permute-start(bf16[128,6144]{1,0:T(8,128)(2,1)S(1)} %collective-permute-done.6), channel_id=1, source_target_pairs={{0,1},{1,2},{2,3},{3,4},{4,5},{5,6},{6,7},{7,8},{8,9},{9,10},{10,1... | collective-permute-start | bytes 4718600 | tf_op jit(solution)/shard_map/ppermute | solution.py:26
  190.2 68.8 %copy-start.30 = (bf16[128,6144]{1,0:T(8,128)(2,1)}, bf16[128,6144]{1,0:T(8,128)(2,1)S(1)}, u32[]{:S(2)}) copy-start(bf16[128,6144]{1,0:T(8,128)(2,1)S(1)} %collective-permute-done.13) | copy-start | bytes 4718596
  190.2 36.6 %collective-permute-start.14 = (bf16[128,6144]{1,0:T(8,128)(2,1)S(1)}, bf16[128,6144]{1,0:T(8,128)(2,1)}, u32[]{:S(2)}, u32[]{:S(2)}) collective-permute-start(bf16[128,6144]{1,0:T(8,128)(2,1)S(1)} %collective-permute-done.13), channel_id=1, source_target_pairs={{1,0},{2,1},{3,2},{4,3},{5,4},{6,5},{7,6},{8,7},{9,8},{10,9},{11,1... | collective-permute-start | bytes 4718600 | tf_op jit(solution)/shard_map/ppermute | solution.py:28
  224.7 34.4 %copy-start.36 = (bf16[128,6144]{1,0:T(8,128)(2,1)}, bf16[128,6144]{1,0:T(8,128)(2,1)S(1)}, u32[]{:S(2)}) copy-start(bf16[128,6144]{1,0:T(8,128)(2,1)S(1)} %collective-permute-done.7) | copy-start | bytes 4718596
  224.7 34.4 %collective-permute-start.8 = (bf16[128,6144]{1,0:T(8,128)(2,1)S(1)}, bf16[128,6144]{1,0:T(8,128)(2,1)}, u32[]{:S(2)}, u32[]{:S(2)}) collective-permute-start(bf16[128,6144]{1,0:T(8,128)(2,1)S(1)} %collective-permute-done.7), channel_id=1, source_target_pairs={{0,1},{1,2},{2,3},{3,4},{4,5},{5,6},{6,7},{7,8},{8,9},{9,10},{10,1... | collective-permute-start | bytes 4718600 | tf_op jit(solution)/shard_map/ppermute | solution.py:26
  226.7 91.8 %collective-permute-start.15 = (bf16[128,6144]{1,0:T(8,128)(2,1)}, bf16[128,6144]{1,0:T(8,128)(2,1)}, u32[]{:S(2)}, u32[]{:S(2)}) collective-permute-start(bf16[128,6144]{1,0:T(8,128)(2,1)} %collective-permute-done.14), channel_id=1, source_target_pairs={{1,0},{2,1},{3,2},{4,3},{5,4},{6,5},{7,6},{8,7},{9,8},{10,9},{11,1... | collective-permute-start | bytes 4718600 | tf_op jit(solution)/shard_map/ppermute | solution.py:28
  259.0 62.3 %collective-permute-start.9 = (bf16[128,6144]{1,0:T(8,128)(2,1)}, bf16[128,6144]{1,0:T(8,128)(2,1)}, u32[]{:S(2)}, u32[]{:S(2)}) collective-permute-start(bf16[128,6144]{1,0:T(8,128)(2,1)} %collective-permute-done.8), channel_id=1, source_target_pairs={{0,1},{1,2},{2,3},{3,4},{4,5},{5,6},{6,7},{7,8},{8,9},{9,10},{10,1... | collective-permute-start | bytes 4718600 | tf_op jit(solution)/shard_map/ppermute | solution.py:26
  318.5 34.8 %collective-permute-start.16 = (bf16[128,6144]{1,0:T(8,128)(2,1)}, bf16[128,6144]{1,0:T(8,128)(2,1)S(1)}, u32[]{:S(2)}, u32[]{:S(2)}) collective-permute-start(bf16[128,6144]{1,0:T(8,128)(2,1)} %collective-permute-done.15), channel_id=1, source_target_pairs={{1,0},{2,1},{3,2},{4,3},{5,4},{6,5},{7,6},{8,7},{9,8},{10,9},{11,1... | collective-permute-start | bytes 4718600 | tf_op jit(solution)/shard_map/ppermute | solution.py:28
  324.0 2.8 copy-start.37
  373.4 32.9 %copy-start.15 = (bf16[1,256,2048]{2,1,0:T(8,128)(2,1)S(1)}, bf16[1,256,2048]{2,1,0:T(8,128)(2,1)}, u32[]{:S(2)}) copy-start(bf16[1,256,2048]{2,1,0:T(8,128)(2,1)} %param.22) | copy-start | bytes 3145732
  373.4 32.9 %copy-start.40 = (f32[1,2048]{1,0:T(1,128)S(1)}, f32[1,2048]{1,0:T(1,128)}, u32[]{:S(2)}) copy-start(f32[1,2048]{1,0:T(1,128)} %param.26) | copy-start | bytes 24580
  803.2 19.1 collective-permute-start
  830.0 19.1 collective-permute-start
  856.9 19.1 collective-permute-start
  883.8 19.3 collective-permute-start
  910.9 20.4 collective-permute-start
  939.0 21.5 collective-permute-start
  968.3 22.6 collective-permute-start
  998.6 23.6 %collective-permute-start = (bf16[2,16,128,128]{3,2,1,0:T(8,128)(2,1)}, bf16[2,16,128,128]{3,2,1,0:T(8,128)(2,1)}, u32[]{:S(2)}, u32[]{:S(2)}) collective-permute-start(bf16[2,16,128,128]{3,2,1,0:T(8,128)(2,1)} %pad_maximum_fusion.4), channel_id=1, source_target_pairs={{0,1},{1,2},{2,3},{3,4},{4,5},{5,6},{6,7},{7,8},{8,9},{9,10},{10,1... | collective-permute-start | bytes 3145736 | tf_op jit(solution)/shard_map/while/body/eval_jaxpr/ppermute | solution.py:38
  1030.0 24.7 %collective-permute-start = (bf16[2,16,128,128]{3,2,1,0:T(8,128)(2,1)}, bf16[2,16,128,128]{3,2,1,0:T(8,128)(2,1)}, u32[]{:S(2)}, u32[]{:S(2)}) collective-permute-start(bf16[2,16,128,128]{3,2,1,0:T(8,128)(2,1)} %pad_maximum_fusion.4), channel_id=1, source_target_pairs={{0,1},{1,2},{2,3},{3,4},{4,5},{5,6},{6,7},{7,8},{8,9},{9,10},{10,1... | collective-permute-start | bytes 3145736 | tf_op jit(solution)/shard_map/while/body/eval_jaxpr/ppermute | solution.py:38
  1062.5 25.8 %collective-permute-start = (bf16[2,16,128,128]{3,2,1,0:T(8,128)(2,1)}, bf16[2,16,128,128]{3,2,1,0:T(8,128)(2,1)}, u32[]{:S(2)}, u32[]{:S(2)}) collective-permute-start(bf16[2,16,128,128]{3,2,1,0:T(8,128)(2,1)} %pad_maximum_fusion.4), channel_id=1, source_target_pairs={{0,1},{1,2},{2,3},{3,4},{4,5},{5,6},{6,7},{7,8},{8,9},{9,10},{10,1... | collective-permute-start | bytes 3145736 | tf_op jit(solution)/shard_map/while/body/eval_jaxpr/ppermute | solution.py:38
  1096.1 26.9 %collective-permute-start = (bf16[2,16,128,128]{3,2,1,0:T(8,128)(2,1)}, bf16[2,16,128,128]{3,2,1,0:T(8,128)(2,1)}, u32[]{:S(2)}, u32[]{:S(2)}) collective-permute-start(bf16[2,16,128,128]{3,2,1,0:T(8,128)(2,1)} %pad_maximum_fusion.4), channel_id=1, source_target_pairs={{0,1},{1,2},{2,3},{3,4},{4,5},{5,6},{6,7},{7,8},{8,9},{9,10},{10,1... | collective-permute-start | bytes 3145736 | tf_op jit(solution)/shard_map/while/body/eval_jaxpr/ppermute | solution.py:38
  1130.7 28.0 %collective-permute-start = (bf16[2,16,128,128]{3,2,1,0:T(8,128)(2,1)}, bf16[2,16,128,128]{3,2,1,0:T(8,128)(2,1)}, u32[]{:S(2)}, u32[]{:S(2)}) collective-permute-start(bf16[2,16,128,128]{3,2,1,0:T(8,128)(2,1)} %pad_maximum_fusion.4), channel_id=1, source_target_pairs={{0,1},{1,2},{2,3},{3,4},{4,5},{5,6},{6,7},{7,8},{8,9},{9,10},{10,1... | collective-permute-start | bytes 3145736 | tf_op jit(solution)/shard_map/while/body/eval_jaxpr/ppermute | solution.py:38
  1166.5 29.1 %collective-permute-start = (bf16[2,16,128,128]{3,2,1,0:T(8,128)(2,1)}, bf16[2,16,128,128]{3,2,1,0:T(8,128)(2,1)}, u32[]{:S(2)}, u32[]{:S(2)}) collective-permute-start(bf16[2,16,128,128]{3,2,1,0:T(8,128)(2,1)} %pad_maximum_fusion.4), channel_id=1, source_target_pairs={{0,1},{1,2},{2,3},{3,4},{4,5},{5,6},{6,7},{7,8},{8,9},{9,10},{10,1... | collective-permute-start | bytes 3145736 | tf_op jit(solution)/shard_map/while/body/eval_jaxpr/ppermute | solution.py:38
  1203.3 30.2 %collective-permute-start = (bf16[2,16,128,128]{3,2,1,0:T(8,128)(2,1)}, bf16[2,16,128,128]{3,2,1,0:T(8,128)(2,1)}, u32[]{:S(2)}, u32[]{:S(2)}) collective-permute-start(bf16[2,16,128,128]{3,2,1,0:T(8,128)(2,1)} %pad_maximum_fusion.4), channel_id=1, source_target_pairs={{0,1},{1,2},{2,3},{3,4},{4,5},{5,6},{6,7},{7,8},{8,9},{9,10},{10,1... | collective-permute-start | bytes 3145736 | tf_op jit(solution)/shard_map/while/body/eval_jaxpr/ppermute | solution.py:38
  1241.3 19.1 collective-permute-start
  1315.4 5.5 copy-start.4
  1324.8 14.5 collective-permute-start.17
  1707.2 2.7 copy-start.6
  1720.8 2.7 copy-start.6
  1755.4 28.5 %collective-permute-start.1 = (bf16[2,16,128,128]{3,2,1,0:T(8,128)(2,1)}, bf16[2,16,128,128]{3,2,1,0:T(8,128)(2,1)}, u32[]{:S(2)}, u32[]{:S(2)}) collective-permute-start(bf16[2,16,128,128]{3,2,1,0:T(8,128)(2,1)} %pad_maximum_fusion.5), channel_id=1, source_target_pairs={{0,1},{1,2},{2,3},{3,4},{4,5},{5,6},{6,7},{7,8},{8,9},{9,10},{10,1... | collective-permute-start | bytes 3145736 | tf_op jit(solution)/shard_map/while/body/eval_jaxpr/ppermute | solution.py:38
  1792.6 27.6 %collective-permute-start.1 = (bf16[2,16,128,128]{3,2,1,0:T(8,128)(2,1)}, bf16[2,16,128,128]{3,2,1,0:T(8,128)(2,1)}, u32[]{:S(2)}, u32[]{:S(2)}) collective-permute-start(bf16[2,16,128,128]{3,2,1,0:T(8,128)(2,1)} %pad_maximum_fusion.5), channel_id=1, source_target_pairs={{0,1},{1,2},{2,3},{3,4},{4,5},{5,6},{6,7},{7,8},{8,9},{9,10},{10,1... | collective-permute-start | bytes 3145736 | tf_op jit(solution)/shard_map/while/body/eval_jaxpr/ppermute | solution.py:38
  1829.0 26.7 %collective-permute-start.1 = (bf16[2,16,128,128]{3,2,1,0:T(8,128)(2,1)}, bf16[2,16,128,128]{3,2,1,0:T(8,128)(2,1)}, u32[]{:S(2)}, u32[]{:S(2)}) collective-permute-start(bf16[2,16,128,128]{3,2,1,0:T(8,128)(2,1)} %pad_maximum_fusion.5), channel_id=1, source_target_pairs={{0,1},{1,2},{2,3},{3,4},{4,5},{5,6},{6,7},{7,8},{8,9},{9,10},{10,1... | collective-permute-start | bytes 3145736 | tf_op jit(solution)/shard_map/while/body/eval_jaxpr/ppermute | solution.py:38
  1864.4 25.8 %collective-permute-start.1 = (bf16[2,16,128,128]{3,2,1,0:T(8,128)(2,1)}, bf16[2,16,128,128]{3,2,1,0:T(8,128)(2,1)}, u32[]{:S(2)}, u32[]{:S(2)}) collective-permute-start(bf16[2,16,128,128]{3,2,1,0:T(8,128)(2,1)} %pad_maximum_fusion.5), channel_id=1, source_target_pairs={{0,1},{1,2},{2,3},{3,4},{4,5},{5,6},{6,7},{7,8},{8,9},{9,10},{10,1... | collective-permute-start | bytes 3145736 | tf_op jit(solution)/shard_map/while/body/eval_jaxpr/ppermute | solution.py:38
  1898.9 24.8 %collective-permute-start.1 = (bf16[2,16,128,128]{3,2,1,0:T(8,128)(2,1)}, bf16[2,16,128,128]{3,2,1,0:T(8,128)(2,1)}, u32[]{:S(2)}, u32[]{:S(2)}) collective-permute-start(bf16[2,16,128,128]{3,2,1,0:T(8,128)(2,1)} %pad_maximum_fusion.5), channel_id=1, source_target_pairs={{0,1},{1,2},{2,3},{3,4},{4,5},{5,6},{6,7},{7,8},{8,9},{9,10},{10,1... | collective-permute-start | bytes 3145736 | tf_op jit(solution)/shard_map/while/body/eval_jaxpr/ppermute | solution.py:38
  1932.5 23.9 %collective-permute-start.1 = (bf16[2,16,128,128]{3,2,1,0:T(8,128)(2,1)}, bf16[2,16,128,128]{3,2,1,0:T(8,128)(2,1)}, u32[]{:S(2)}, u32[]{:S(2)}) collective-permute-start(bf16[2,16,128,128]{3,2,1,0:T(8,128)(2,1)} %pad_maximum_fusion.5), channel_id=1, source_target_pairs={{0,1},{1,2},{2,3},{3,4},{4,5},{5,6},{6,7},{7,8},{8,9},{9,10},{10,1... | collective-permute-start | bytes 3145736 | tf_op jit(solution)/shard_map/while/body/eval_jaxpr/ppermute | solution.py:38
  1965.1 23.0 %collective-permute-start.1 = (bf16[2,16,128,128]{3,2,1,0:T(8,128)(2,1)}, bf16[2,16,128,128]{3,2,1,0:T(8,128)(2,1)}, u32[]{:S(2)}, u32[]{:S(2)}) collective-permute-start(bf16[2,16,128,128]{3,2,1,0:T(8,128)(2,1)} %pad_maximum_fusion.5), channel_id=1, source_target_pairs={{0,1},{1,2},{2,3},{3,4},{4,5},{5,6},{6,7},{7,8},{8,9},{9,10},{10,1... | collective-permute-start | bytes 3145736 | tf_op jit(solution)/shard_map/while/body/eval_jaxpr/ppermute | solution.py:38
  1996.9 22.1 collective-permute-start.1
  2027.7 21.1 collective-permute-start.1
  2057.6 20.2 collective-permute-start.1
  2086.6 19.3 collective-permute-start.1
  2114.6 19.1 collective-permute-start.1
  2142.5 19.1 collective-permute-start.1
  2170.3 19.1 collective-permute-start.1
  2198.2 19.1 collective-permute-start.1
  2220.1 4.0 copy-start.10
  2267.7 3.9 copy-start.1
  (68 other events, 151.4 us)
Sparse Core Ops, SparseCore 0:
  1327.7 90.4 all-reduce.2
